TPU v7x, 512 devices: a whole 4x4x16 slice. The times are simulated.
512 devices in a mesh: clu: 64 (over z, y), col: 8 (over x, core).
Axes of the slice: x: 4, y: 4, z: 16, core: 2. Of those that a mesh axis runs over, the one named last changes fastest.
Arguments:
- near_blocks: float32 [64, 16, 512, 512], P('clu', 'col'), may hold values from -0.25 to 0.25
- diag_block: float32 [64, 512, 512], P('clu', 'col'), as said below
- bases: float32 [64, 512, 512], P('clu', 'col'), as said below
- near_index: int32 [64, 16], replicated, may hold values from 0 to 63, as said below
- near_mask: int32 [64, 16], P('clu'), may hold values from 0 to 1
- parent_map: int32 [64], replicated, may hold values from 0 to 31, as said below
Outputs:
- coupling: float32 [64, 16, 256, 256], P('clu', 'col')
- parent_rows: float32 [64, 256, 512], P('clu', 'col')
- redundant_factor: float32 [64, 256, 256], P('clu', 'col')
Inputs may be any that keep to these rules, and one draw needn't show every extreme that they name: `parent_map`: every parent has exactly two children. `near_index`: the slots of cluster i name the clusters (i + d) mod 64 for d = 1 to 7, d = 32 and d = -1 to -8, each offset in exactly one slot, in an order drawn per row; live slots name distinct clusters; exactly one live slot names the cluster's sibling. `diag_block`: each block is symmetric and positive definite. `bases`: each basis change is invertible.
All inputs are finite; a program needn't handle non-finite values.
Results may differ from a plain program's by a relative error of at most 0.0003.
Values sent between devices are 32-bit elements; how exact they have to be, the bound alone decides.
No kernel may reach another device: no remote copies, remote signals or barrier semaphores. Data moves between devices by JAX's collectives and lax.ppermute only.
A program may use at most 64 MiB of HBM per device.

v0:
```python
import jax
import jax.numpy as jnp
from jax import lax
from jax.sharding import PartitionSpec as P

RANK = 256


def solve_lower(factor):
    size = factor.shape[0]
    return lax.linalg.triangular_solve(
        factor, jnp.eye(size, dtype=factor.dtype), left_side=True, lower=True
    )


def pick_rows(listed, carry, piece):
    count = piece.shape[0]
    select = (listed[:, None] == jnp.arange(count, dtype=jnp.int32)[None, :]).astype(jnp.float32)
    flat = piece.reshape(count, -1)
    return jnp.dot(select, flat, precision=lax.Precision.HIGHEST).reshape(carry.shape)


def shards(near_blocks, diag_block, bases, near_index, near_mask, parent_map):
    highest = lax.Precision.HIGHEST
    columns = lax.axis_size("col")
    column = lax.axis_index("col")
    own_index = lax.axis_index("clu")
    row_count = bases.shape[1]
    leaf_size = bases.shape[2]
    redundant = leaf_size - RANK
    per_device = near_blocks.shape[1]
    slot_total = near_index.shape[1]
    listed = lax.dynamic_slice_in_dim(near_index, own_index, 1, 0)[0]
    full_diag, full_basis = (
        lax.all_gather(diag_block, "col", axis=1, tiled=True),
        lax.all_gather(bases, "col", axis=1, tiled=True),
    )
    basis = full_basis[0]
    reduced = jnp.dot(basis.T, jnp.dot(full_diag[0], basis, precision=highest), precision=highest)
    factor = jnp.linalg.cholesky(reduced[:redundant, :redundant])
    inverse = solve_lower(factor)
    couple = jnp.dot(inverse, reduced[:redundant, redundant:], precision=highest)
    schur = reduced[redundant:, redundant:] - jnp.dot(couple.T, couple, precision=highest)
    skeleton_rows = bases[:, :, redundant:]
    empty = jnp.zeros((slot_total, row_count, RANK), jnp.float32)
    picked = pick_rows(listed, empty, lax.all_gather(skeleton_rows, "clu", axis=0, tiled=True))
    grouped = picked.reshape(columns, per_device, row_count, RANK)
    routed = lax.all_to_all(grouped, "col", split_axis=0, concat_axis=2, tiled=True)
    partners = routed[0]
    middle = jnp.einsum("kab,kbr->kar", near_blocks[0], partners, precision=highest)
    coupled = jnp.einsum("ba,kbr->kar", basis, middle, precision=highest)
    solved = jnp.einsum("xy,kyr->kxr", inverse, coupled[:, :redundant], precision=highest)
    local_list = lax.dynamic_slice_in_dim(listed, column * per_device, per_device, 0)
    local_live = lax.dynamic_slice_in_dim(near_mask[0], column * per_device, per_device, 0).astype(
        jnp.float32
    )
    coupling = (
        coupled[:, redundant:] - jnp.einsum("xs,kxr->ksr", couple, solved, precision=highest)
    ) * local_live[:, None, None]
    cluster_ids = jnp.arange(parent_map.shape[0], dtype=jnp.int32)
    own_parent = lax.dynamic_slice_in_dim(parent_map, own_index, 1, 0)[0]
    same = (parent_map == own_parent) & (cluster_ids != own_index)
    sibling = jnp.sum(jnp.where(same, cluster_ids, 0))
    matches = local_live * (local_list == sibling).astype(jnp.float32)
    side = jnp.einsum("k,kab->ab", matches, coupling, precision=highest)
    first = (own_index < sibling).astype(jnp.float32)
    side_wide = jnp.concatenate([(1.0 - first) * side, first * side], axis=1)
    summed = lax.psum_scatter(side_wide, "col", scatter_dimension=0, tiled=True)
    merged_count = summed.shape[0]
    schur_rows = lax.dynamic_slice_in_dim(schur, column * merged_count, merged_count, 0)
    parent_rows = summed + jnp.concatenate([first * schur_rows, (1.0 - first) * schur_rows], axis=1)
    factor_count = redundant // columns
    factor_rows = lax.dynamic_slice_in_dim(factor, column * factor_count, factor_count, 0)
    return (coupling[None], parent_rows[None], factor_rows[None])


def solution(mesh):
    in_specs = (
        P("clu", "col", None, None),
        P("clu", "col", None),
        P("clu", "col", None),
        P(),
        P("clu", None),
        P(),
    )
    out_specs = (P("clu", "col", None, None), P("clu", "col", None), P("clu", "col", None))
    return jax.shard_map(shards, mesh=mesh, in_specs=in_specs, out_specs=out_specs, check_vma=False)
```

profile of v0, /device:TPU:8, one launch (start us, length us, event | category | flops | bytes accessed | tf_op | source)
XLA Modules:
  0.0 305.6 jit_solution(5359909306304034356)
XLA Ops:
  7.2 0.0 copy-start
  7.2 0.0 all-gather.6.cloned.1.call-start
  7.2 0.7 all-gather.6.cloned.1.call-update
  7.9 0.0 all-gather.8.cloned.1.call-start
  8.0 0.7 all-gather.8.cloned.1.call-update
  8.7 0.0 all-gather.4.cloned.1.call-start
  8.7 1.5 slice.61
  10.2 0.0 all-gather.4.cloned.1.call-update
  10.2 1.2 dynamic_slice.20
  11.5 0.9 dynamic-slice_reduce_fusion
  12.4 0.1 eq.51
  12.4 0.1 copy.36
  12.5 1.9 fusion.34
  15.1 1.5 compare_reduce_fusion
  16.7 0.6 iota_multiply_fusion
  17.3 0.6 iota_compare_fusion
  17.9 0.7 broadcast_select_fusion
  18.6 26.8 %all-gather.6.cloned.1.call-done = f32[1,512,512]{2,1,0:T(8,128)} async-done(((f32[1,64,512]{2,1,0:T(8,128)}), f32[1,512,512]{2,1,0:T(8,128)}) %all-gather.6.cloned.1.call-update) | async-done | bytes 1048592 | tf_op jit(solution)/shard_map/all_gather | solution.py:36
  45.4 33.0 %all-gather.8.cloned.1.call-done = f32[1,512,512]{2,1,0:T(8,128)} async-done(((f32[1,64,512]{2,1,0:T(8,128)}), f32[1,512,512]{2,1,0:T(8,128)}) %all-gather.8.cloned.1.call-update) | async-done | bytes 1048592 | tf_op jit(solution)/shard_map/all_gather | solution.py:35
  78.5 3.4 %fusion.9 = f32[512,512]{1,0:T(8,128)S(1)} fusion(f32[1,512,512]{2,1,0:T(8,128)} %all-gather.8.cloned.1.call-done, f32[1,512,512]{2,1,0:T(8,128)} %all-gather.6.cloned.1.call-done), kind=kOutput, calls=%fused_computation.16 | convolution fusion | flops 1610612736 | bytes 3145728 | tf_op jit(solution)/shard_map/dot_general | solution.py:39
  81.9 3.1 %convolution_bitcast_fusion = f32[512,512]{0,1:T(8,128)S(1)} fusion(f32[512,512]{1,0:T(8,128)S(1)} %fusion.9, f32[1,512,512]{2,1,0:T(8,128)} %all-gather.6.cloned.1.call-done), kind=kOutput, calls=%fused_computation.8 | convolution fusion | flops 1610612736 | bytes 3145728 | tf_op jit(solution)/shard_map/dot_general | solution.py:39
  84.9 0.0 copy-start.2
  84.9 0.9 fusion.39
  85.9 1.1 copy.42
  87.0 0.7 copy-done.6
  87.7 11.7 %cholesky.50 = f32[128,128]{1,0:T(8,128)S(1)} custom-call(f32[128,128]{1,0:T(8,128)S(1)} %cholesky.118), custom_call_target="Cholesky" | custom-call | tf_op jit(solution)/shard_map/jit(cholesky)/cholesky | solution.py:40
  99.5 9.8 %custom-call.14 = f32[1,128,128]{1,2,0:T(8,128)S(1)} custom-call(f32[1,128,128]{2,1,0:T(8,128)S(1)} %get-tuple-element.46), custom_call_target="InvertDiagBlocksLowerTriangular" | custom-call | tf_op jit(solution)/shard_map/jit(cholesky)/cholesky | solution.py:40
  109.3 1.0 constant_dynamic-update-slice_fusion
  110.4 1.1 convolution_subtract_fusion.1
  111.5 11.9 %cholesky.105 = f32[128,128]{1,0:T(8,128)S(1)} custom-call(f32[128,128]{1,0:T(8,128)S(1)} %convolution_subtract_fusion.1), custom_call_target="Cholesky" | custom-call | tf_op jit(solution)/shard_map/jit(cholesky)/cholesky | solution.py:40
  123.4 0.7 compare_reduce_fusion.1
  125.3 1.7 fusion.21
  127.0 0.7 triangular_solve.63
  127.8 5.3 %while.1 = (s32[]{:T(128)}, f32[256,256]{1,0:T(8,128)S(1)}, s32[2,2]{1,0:T(2,128)S(1)}, f32[2,128,128]{2,1,0:T(8,128)}, s32[]{:T(128)}) while((s32[]{:T(128)}, f32[256,256]{1,0:T(8,128)S(1)}, s32[2,2]{1,0:T(2,128)S(1)}, f32[2,128,128]{2,1,0:T(8,128)}, s32[]{:T(128)}) %tuple.37), condition=%wide.while_cond, body=%wide.while_body.sunk | while | flops 2 | bytes 132205 | solution.py:11
  127.8 0.6 fusion.52
  128.4 2.0 bitcast_dynamic-update-slice_fusion.2
  130.4 0.6 fusion.52
  131.0 2.0 bitcast_dynamic-update-slice_fusion.2
  133.0 21.1 %custom-call.15 = f32[2,128,128]{1,2,0:T(8,128)} custom-call(f32[2,128,128]{2,1,0:T(8,128)} %get-tuple-element.10), custom_call_target="InvertDiagBlocksLowerTriangular" | custom-call | tf_op jit(solution)/shard_map/triangular_solve | solution.py:11
  154.1 72.9 %all-gather.4.cloned.1.call-done = f32[64,64,256]{2,1,0:T(8,128)} async-done(((f32[1,64,256]{2,1,0:T(8,128)}), f32[64,64,256]{2,1,0:T(8,128)}) %all-gather.4.cloned.1.call-update) | async-done | bytes 4194320 | tf_op jit(solution)/shard_map/all_gather | solution.py:46
  227.1 5.8 %fusion = f32[8,2,64,256]{3,0,2,1:T(8,128)S(1)} fusion(s32[8,2]{0,1:T(2,128)S(1)} %copy.36, f32[8,8,64,256]{3,2,1,0:T(8,128)} %bitcast.110), kind=kOutput, calls=%fused_computation.3 | convolution fusion | flops 201327616 | bytes 5242944 | tf_op jit(solution)/shard_map/dot_general | solution.py:20
  232.9 1.4 copy.38
  234.3 4.3 %all-to-all-start = ((f32[8,2,64,256]{3,2,1,0:T(8,128)}), f32[8,2,64,256]{3,2,1,0:T(8,128)}, u32[]{:S(2)}, u32[]{:S(2)}) async-start(f32[8,2,64,256]{3,2,1,0:T(8,128)} %copy.38), calls=%async_computation | async-start | bytes 2097152 | tf_op jit(solution)/shard_map/all_to_all | solution.py:48
  238.5 0.3 reduce-scatter.4.cloned.1.call-start
  238.8 1.1 fusion.22
  239.9 1.0 convolution_subtract_fusion
  241.0 1.1 fusion.25
  242.1 0.6 copy-done.3
  242.8 1.4 fusion.15
  244.1 10.4 %all-to-all-done = f32[8,2,64,256]{3,2,1,0:T(8,128)} async-done(((f32[8,2,64,256]{3,2,1,0:T(8,128)}), f32[8,2,64,256]{3,2,1,0:T(8,128)}, u32[]{:S(2)}, u32[]{:S(2)}) %all-to-all-start) | async-done | bytes 1048608 | tf_op jit(solution)/shard_map/all_to_all | solution.py:48
  254.6 1.3 copy.39
  255.9 3.6 %fusion.4 = f32[2,512,256]{1,2,0:T(8,128)S(1)} fusion(f32[2,512,256]{2,1,0:T(8,128)S(1)} %bitcast.111, f32[1,2,512,512]{3,2,1,0:T(8,128)S(1)} %copy-done), kind=kOutput, calls=%fused_computation.7 | convolution fusion | flops 1610612736 | bytes 4194304 | tf_op jit(solution)/shard_map/kab,kbr->kar/dot_general | solution.py:50
  259.5 1.9 convolution_bitcast_fusion.1
  261.4 0.6 convolution_bitcast_fusion.3
  262.0 0.6 multiply_reduce_fusion
  262.7 1.0 copy.53
  263.7 0.0 reduce-scatter.4.cloned.1.call-update
  263.7 1.4 dynamic-slice_bitcast_fusion
  265.1 0.6 fusion.40
  265.7 1.0 broadcast_multiply_fusion.3
  266.8 1.0 copy.44
  267.8 29.6 %reduce-scatter.4.cloned.1.call-done = f32[32,512]{1,0:T(8,128)} async-done(((f32[256,512]{1,0:T(8,128)}), f32[32,512]{1,0:T(8,128)}) %reduce-scatter.4.cloned.1.call-update) | async-done | bytes 65552
  297.4 1.0 copy.54
  298.4 0.7 copy.45
  (21 shorter events, 0.3 us)
Async XLA Ops:
  7.2 248.7 %copy-start = (f32[1,2,512,512]{3,2,1,0:T(8,128)S(1)}, f32[1,2,512,512]{3,2,1,0:T(8,128)}, u32[]{:S(2)}) copy-start(f32[1,2,512,512]{3,2,1,0:T(8,128)} %param.6) | copy-start | bytes 6291460
  7.2 38.3 %all-gather.6.cloned.1.call-start = ((), (), s32[]{:S(2)}) async-start(), calls=%async_computation.3 | async-start | bytes 1179648 | tf_op jit(solution)/shard_map/all_gather | solution.py:36
  7.9 70.6 %all-gather.8.cloned.1.call-start = ((), (), s32[]{:S(2)}) async-start(), calls=%async_computation.4 | async-start | bytes 1179648 | tf_op jit(solution)/shard_map/all_gather | solution.py:35
  8.7 218.4 %all-gather.4.cloned.1.call-start = ((), (), s32[]{:S(2)}) async-start(), calls=%async_computation.2 | async-start | bytes 4259840 | tf_op jit(solution)/shard_map/all_gather | solution.py:46
  84.9 148.0 %copy-start.2 = (f32[512,512]{0,1:T(8,128)}, f32[512,512]{0,1:T(8,128)S(1)}, u32[]{:S(2)}) copy-start(f32[512,512]{0,1:T(8,128)S(1)} %convolution_bitcast_fusion) | copy-start | bytes 3145732
  87.0 0.7 copy-start.6
  123.4 2.0 copy-start.5
  234.3 20.3 %all-to-all-start = ((f32[8,2,64,256]{3,2,1,0:T(8,128)}), f32[8,2,64,256]{3,2,1,0:T(8,128)}, u32[]{:S(2)}, u32[]{:S(2)}) async-start(f32[8,2,64,256]{3,2,1,0:T(8,128)} %copy.38), calls=%async_computation | async-start | bytes 2097152 | tf_op jit(solution)/shard_map/all_to_all | solution.py:48
  238.5 21.0 %copy-start.1 = (f32[1,512,512]{2,1,0:T(8,128)S(1)}, f32[1,512,512]{2,1,0:T(8,128)}, u32[]{:S(2)}) copy-start(f32[1,512,512]{2,1,0:T(8,128)} %all-gather.6.cloned.1.call-done) | copy-start | bytes 3145732
  238.5 58.8 %reduce-scatter.4.cloned.1.call-start = ((), (), s32[]{:S(2)}) async-start(), calls=%async_computation.5 | async-start | bytes 589824
  242.1 0.7 copy-start.3
  255.9 5.5 %copy-start.4 = (f32[128,256]{1,0:T(8,128)S(1)}, f32[128,256]{1,0:T(8,128)}, u32[]{:S(2)}) copy-start(f32[128,256]{1,0:T(8,128)} %copy-done.3) | copy-start | bytes 393220
Sparse Core Ops, SparseCore 0:
  10.1 35.2 all-gather.5
  47.6 30.8 all-gather.7
  82.0 145.0 all-gather.3
  263.8 33.4 reduce-scatter.3
where the time goes:
time: 307 us; the launch traced here: 306 us
  waiting for transfers between devices  174 us (57%)
  other arithmetic  63.5 us (21%)
  matrix products  26.3 us (9%)
  local copies, waits for them, and re-layouts  20.9 us (7%)
  between operations  16 us (5%)
  starting transfers between devices  4.63 us (2%)
    all_gather x1, waiting for transfers between devices, shards(): lax.all_gather(skeleton_rows, 'clu', axis=0, tiled=True)  72.9 us
    another operation x6, other arithmetic, shards(): factor = jnp.linalg.cholesky(reduced[:redundant, :redundant])  34.1 us
    all_gather x1, waiting for transfers between devices, shards(): lax.all_gather(diag_block, 'col', axis=1, tiled=True)  33 us
    unnamed x5, waiting for transfers between devices  31 us
    all_gather x1, waiting for transfers between devices, shards(): lax.all_gather(bases, 'col', axis=1, tiled=True)  26.8 us
    another operation x3, other arithmetic, solve_lower(): lax.linalg.triangular_solve(factor, jnp.eye(size, dtype=factor.dtype), le...  23.4 us
    all_to_all x1, waiting for transfers between devices, shards(): lax.all_to_all(grouped, 'col', split_axis=0, concat_axis=2, tiled=True)  10.4 us
  transfers between devices with their start and end apart: 5, of which 5 were waited for; matrix products, arithmetic and copies ran while one was open for 30% of the time, Pallas kernels for 0%

commit v1 on v0

--- a/solution.py
+++ b/solution.py
@@ -33,7 +33,9 @@
     listed = lax.dynamic_slice_in_dim(near_index, own_index, 1, 0)[0]
     full_diag, full_basis = (
         lax.all_gather(diag_block, "col", axis=1, tiled=True),
-        lax.all_gather(bases, "col", axis=1, tiled=True),
+        jnp.concatenate(
+            lax.all_to_all(jnp.stack([bases] * lax.axis_size("col")), "col", 0, 0), axis=1
+        ),
     )
     basis = full_basis[0]
     reduced = jnp.dot(basis.T, jnp.dot(full_diag[0], basis, precision=highest), precision=highest)

time: 307 us -> 273 us (0.89)
  waiting for transfers between devices: 174 us -> 135 us
  starting transfers between devices: 4.63 us -> 8.89 us
    all_gather x1 -> x0, waiting for transfers between devices: 26.8 us -> none  [shards(): lax.all_gather(bases, 'col', axis=1, tiled=True)]
    all_gather x1, waiting for transfers between devices: 33 us -> 13.7 us  [shards(): lax.all_gather(diag_block, 'col', axis=1, tiled=True)]
    all_to_all x0 -> x1, waiting for transfers between devices: none -> 7.6 us  [shards(): lax.all_to_all(jnp.stack([bases] * lax.axis_size('col')), 'col', 0, 0)]
    all_to_all x0 -> x1, starting transfers between devices: none -> 4.3 us  [shards(): lax.all_to_all(jnp.stack([bases] * lax.axis_size('col')), 'col', 0, 0)]
    another operation x6 -> x7, local copies, waits for them, and re-layouts: 5.27 us -> 7.09 us
    unnamed x5 -> x4, waiting for transfers between devices: 31 us -> 30.2 us
  transfers between devices with their start and end apart: 5 -> 5, of which waited for: 5 -> 5; matrix products, arithmetic and copies ran while one was open for 30% -> 34% of each run, Pallas kernels for 0% -> 0%
where the time goes in v1:
time: 273 us; the launch traced here: 272 us
  waiting for transfers between devices  135 us (49%)
  other arithmetic  64.4 us (24%)
  matrix products  24.8 us (9%)
  local copies, waits for them, and re-layouts  23.5 us (9%)
  between operations  15.9 us (6%)
  starting transfers between devices  8.89 us (3%)
    all_gather x1, waiting for transfers between devices, shards(): lax.all_gather(skeleton_rows, 'clu', axis=0, tiled=True)  72.8 us
    another operation x6, other arithmetic, shards(): factor = jnp.linalg.cholesky(reduced[:redundant, :redundant])  34.1 us
    unnamed x4, waiting for transfers between devices  30.2 us
    another operation x3, other arithmetic, solve_lower(): lax.linalg.triangular_solve(factor, jnp.eye(size, dtype=factor.dtype), le...  23.3 us
    all_gather x1, waiting for transfers between devices, shards(): lax.all_gather(diag_block, 'col', axis=1, tiled=True)  13.7 us
    all_to_all x1, waiting for transfers between devices, shards(): lax.all_to_all(grouped, 'col', split_axis=0, concat_axis=2, tiled=True)  10.5 us
    all_to_all x1, waiting for transfers between devices, shards(): lax.all_to_all(jnp.stack([bases] * lax.axis_size('col')), 'col', 0, 0)  7.6 us
    unnamed x16, local copies, waits for them, and re-layouts  6.01 us
  transfers between devices with their start and end apart: 5, of which 5 were waited for; matrix products, arithmetic and copies ran while one was open for 34% of the time, Pallas kernels for 0%

profile of v1, /device:TPU:8, one launch (start us, length us, event | category | flops | bytes accessed | tf_op | source)
XLA Modules:
  0.0 272.3 jit_solution(15328348103734469699)
XLA Ops:
  7.2 0.0 all-gather.5.cloned.1.call-start
  7.2 0.7 all-gather.5.cloned.1.call-update
  7.9 0.0 all-gather.3.cloned.1.call-start
  8.0 1.5 slice.61
  9.4 0.0 all-gather.3.cloned.1.call-update
  9.5 2.0 stack.2
  11.5 4.3 %all-to-all-start.1 = ((f32[8,1,64,512]{3,2,1,0:T(8,128)}), f32[8,1,64,512]{3,2,1,0:T(8,128)S(1)}, u32[]{:S(2)}, u32[]{:S(2)}) async-start(f32[8,1,64,512]{3,2,1,0:T(8,128)} %stack.2), calls=%async_computation.1 | async-start | bytes 2097152 | tf_op jit(solution)/shard_map/all_to_all | solution.py:37
  15.8 1.2 dynamic_slice.20
  17.0 0.9 dynamic-slice_reduce_fusion
  17.9 0.1 eq.51
  18.0 0.1 copy.36
  18.1 1.9 fusion.31
  20.7 1.5 compare_reduce_fusion
  22.2 0.5 iota_multiply_fusion
  22.8 0.7 iota_compare_fusion
  23.4 0.7 broadcast_select_fusion
  24.1 7.6 %all-to-all-done.1 = f32[8,1,64,512]{3,2,1,0:T(8,128)S(1)} async-done(((f32[8,1,64,512]{3,2,1,0:T(8,128)}), f32[8,1,64,512]{3,2,1,0:T(8,128)S(1)}, u32[]{:S(2)}, u32[]{:S(2)}) %all-to-all-start.1) | async-done | bytes 1048608 | tf_op jit(solution)/shard_map/all_to_all | solution.py:37
  31.7 13.7 %all-gather.5.cloned.1.call-done = f32[1,512,512]{2,1,0:T(8,128)} async-done(((f32[1,64,512]{2,1,0:T(8,128)}), f32[1,512,512]{2,1,0:T(8,128)}) %all-gather.5.cloned.1.call-update) | async-done | bytes 1048592 | tf_op jit(solution)/shard_map/all_gather | solution.py:35
  45.4 3.1 %fusion.9 = f32[512,512]{1,0:T(8,128)S(1)} fusion(f32[512,512]{1,0:T(8,128)S(1)} %bitcast.109, f32[1,512,512]{2,1,0:T(8,128)} %all-gather.5.cloned.1.call-done), kind=kOutput, calls=%fused_computation.16 | convolution fusion | flops 1610612736 | bytes 3145728 | tf_op jit(solution)/shard_map/dot_general | solution.py:41
  48.5 1.8 convolution_bitcast_fusion
  50.4 1.0 copy-done.1
  51.3 0.8 fusion.36
  52.2 1.1 copy.42
  53.2 1.0 fusion.17
  54.2 0.7 copy-done.5
  54.9 11.7 %cholesky.50 = f32[128,128]{1,0:T(8,128)S(1)} custom-call(f32[128,128]{1,0:T(8,128)S(1)} %cholesky.118), custom_call_target="Cholesky" | custom-call | tf_op jit(solution)/shard_map/jit(cholesky)/cholesky | solution.py:42
  66.7 9.8 %custom-call.14 = f32[1,128,128]{1,2,0:T(8,128)S(1)} custom-call(f32[1,128,128]{2,1,0:T(8,128)S(1)} %get-tuple-element.46), custom_call_target="InvertDiagBlocksLowerTriangular" | custom-call | tf_op jit(solution)/shard_map/jit(cholesky)/cholesky | solution.py:42
  76.5 1.0 constant_dynamic-update-slice_fusion
  77.6 1.1 convolution_subtract_fusion.1
  78.7 11.9 %cholesky.105 = f32[128,128]{1,0:T(8,128)S(1)} custom-call(f32[128,128]{1,0:T(8,128)S(1)} %convolution_subtract_fusion.1), custom_call_target="Cholesky" | custom-call | tf_op jit(solution)/shard_map/jit(cholesky)/cholesky | solution.py:42
  90.6 0.7 compare_reduce_fusion.1
  92.5 1.7 fusion.18
  94.2 0.7 triangular_solve.63
  94.9 5.0 %while.1 = (s32[]{:T(128)}, f32[256,256]{1,0:T(8,128)S(1)}, s32[2,2]{1,0:T(2,128)S(1)}, f32[2,128,128]{2,1,0:T(8,128)}, s32[]{:T(128)}) while((s32[]{:T(128)}, f32[256,256]{1,0:T(8,128)S(1)}, s32[2,2]{1,0:T(2,128)S(1)}, f32[2,128,128]{2,1,0:T(8,128)}, s32[]{:T(128)}) %tuple.37), condition=%wide.while_cond, body=%wide.while_body.sunk | while | flops 2 | bytes 132205 | solution.py:11
  94.9 0.6 fusion.52
  95.5 1.9 bitcast_dynamic-update-slice_fusion.2
  97.4 0.6 fusion.52
  98.0 1.9 bitcast_dynamic-update-slice_fusion.2
  99.9 21.1 %custom-call.15 = f32[2,128,128]{1,2,0:T(8,128)} custom-call(f32[2,128,128]{2,1,0:T(8,128)} %get-tuple-element.10), custom_call_target="InvertDiagBlocksLowerTriangular" | custom-call | tf_op jit(solution)/shard_map/triangular_solve | solution.py:11
  121.0 72.8 %all-gather.3.cloned.1.call-done = f32[64,64,256]{2,1,0:T(8,128)} async-done(((f32[1,64,256]{2,1,0:T(8,128)}), f32[64,64,256]{2,1,0:T(8,128)}) %all-gather.3.cloned.1.call-update) | async-done | bytes 4194320 | tf_op jit(solution)/shard_map/all_gather | solution.py:48
  193.8 5.8 %fusion = f32[8,2,64,256]{3,0,2,1:T(8,128)S(1)} fusion(s32[8,2]{0,1:T(2,128)S(1)} %copy.36, f32[8,8,64,256]{3,2,1,0:T(8,128)} %bitcast.112), kind=kOutput, calls=%fused_computation.3 | convolution fusion | flops 201327616 | bytes 5242944 | tf_op jit(solution)/shard_map/dot_general | solution.py:20
  199.7 1.3 copy.38
  201.0 4.3 %all-to-all-start = ((f32[8,2,64,256]{3,2,1,0:T(8,128)}), f32[8,2,64,256]{3,2,1,0:T(8,128)}, u32[]{:S(2)}, u32[]{:S(2)}) async-start(f32[8,2,64,256]{3,2,1,0:T(8,128)} %copy.38), calls=%async_computation | async-start | bytes 2097152 | tf_op jit(solution)/shard_map/all_to_all | solution.py:50
  205.2 0.3 reduce-scatter.4.cloned.1.call-start
  205.5 1.1 fusion.19
  206.6 1.0 convolution_subtract_fusion
  207.7 1.1 fusion.22
  208.8 0.6 copy-done.2
  209.5 1.4 fusion.12
  210.8 10.5 %all-to-all-done = f32[8,2,64,256]{3,2,1,0:T(8,128)} async-done(((f32[8,2,64,256]{3,2,1,0:T(8,128)}), f32[8,2,64,256]{3,2,1,0:T(8,128)}, u32[]{:S(2)}, u32[]{:S(2)}) %all-to-all-start) | async-done | bytes 1048608 | tf_op jit(solution)/shard_map/all_to_all | solution.py:50
  221.3 1.3 copy.39
  222.6 3.6 %fusion.4 = f32[2,512,256]{1,2,0:T(8,128)S(1)} fusion(f32[2,512,256]{2,1,0:T(8,128)S(1)} %bitcast.113, f32[1,2,512,512]{3,2,1,0:T(8,128)S(1)} %copy-done), kind=kOutput, calls=%fused_computation.7 | convolution fusion | flops 1610612736 | bytes 4194304 | tf_op jit(solution)/shard_map/kab,kbr->kar/dot_general | solution.py:52
  226.2 1.9 convolution_bitcast_fusion.1
  228.1 0.6 convolution_bitcast_fusion.3
  228.7 0.6 multiply_reduce_fusion
  229.4 1.0 copy.53
  230.4 0.0 reduce-scatter.4.cloned.1.call-update
  230.4 1.4 dynamic-slice_bitcast_fusion
  231.8 0.6 fusion.37
  232.4 1.0 broadcast_multiply_fusion.3
  233.5 1.0 copy.44
  234.5 29.5 %reduce-scatter.4.cloned.1.call-done = f32[32,512]{1,0:T(8,128)} async-done(((f32[256,512]{1,0:T(8,128)}), f32[32,512]{1,0:T(8,128)}) %reduce-scatter.4.cloned.1.call-update) | async-done | bytes 65552
  264.0 1.0 copy.54
  265.0 0.7 copy.45
  (19 shorter events, 0.2 us)
Async XLA Ops:
  7.2 215.4 %copy-start = (f32[1,2,512,512]{3,2,1,0:T(8,128)S(1)}, f32[1,2,512,512]{3,2,1,0:T(8,128)}, u32[]{:S(2)}) copy-start(f32[1,2,512,512]{3,2,1,0:T(8,128)} %param.6) | copy-start | bytes 6291460
  7.2 38.3 %all-gather.5.cloned.1.call-start = ((), (), s32[]{:S(2)}) async-start(), calls=%async_computation.4 | async-start | bytes 1179648 | tf_op jit(solution)/shard_map/all_gather | solution.py:35
  7.9 185.9 %all-gather.3.cloned.1.call-start = ((), (), s32[]{:S(2)}) async-start(), calls=%async_computation.3 | async-start | bytes 4259840 | tf_op jit(solution)/shard_map/all_gather | solution.py:48
  11.5 20.2 %all-to-all-start.1 = ((f32[8,1,64,512]{3,2,1,0:T(8,128)}), f32[8,1,64,512]{3,2,1,0:T(8,128)S(1)}, u32[]{:S(2)}, u32[]{:S(2)}) async-start(f32[8,1,64,512]{3,2,1,0:T(8,128)} %stack.2), calls=%async_computation.1 | async-start | bytes 2097152 | tf_op jit(solution)/shard_map/all_to_all | solution.py:37
  50.4 1.0 copy-start.1
  54.2 0.7 copy-start.5
  90.6 1.9 copy-start.4
  201.0 20.3 %all-to-all-start = ((f32[8,2,64,256]{3,2,1,0:T(8,128)}), f32[8,2,64,256]{3,2,1,0:T(8,128)}, u32[]{:S(2)}, u32[]{:S(2)}) async-start(f32[8,2,64,256]{3,2,1,0:T(8,128)} %copy.38), calls=%async_computation | async-start | bytes 2097152 | tf_op jit(solution)/shard_map/all_to_all | solution.py:50
  205.2 58.7 %reduce-scatter.4.cloned.1.call-start = ((), (), s32[]{:S(2)}) async-start(), calls=%async_computation.5 | async-start | bytes 589824
  208.8 0.7 copy-start.2
  222.6 5.5 %copy-start.3 = (f32[128,256]{1,0:T(8,128)S(1)}, f32[128,256]{1,0:T(8,128)}, u32[]{:S(2)}) copy-start(f32[128,256]{1,0:T(8,128)} %copy-done.2) | copy-start | bytes 393220
Sparse Core Ops, SparseCore 0:
  10.1 35.2 all-gather.4
  49.0 144.8 all-gather.2
  230.6 33.3 reduce-scatter.3
